TPU v7x, 512 devices: a whole 4x8x8 slice. The times are simulated.
512 devices in a mesh: ctx: 64 (over z, y), head: 8 (over x, core).
Axes of the slice: x: 4, y: 8, z: 8, core: 2. Of those that a mesh axis runs over, the one named last changes fastest.
Arguments:
- token_inputs: bfloat16 [32768, 8192], P(('ctx', 'head')), may hold values from -6 to 6
- state_in: bfloat16 [32768, 128], P(('ctx', 'head')), may hold values from -0.059814453 to 0.059814453
- state_out: bfloat16 [32768, 128], P(('ctx', 'head')), may hold values from -0.5 to 0.5
- log_decay: bfloat16 [32768, 128], P(('ctx', 'head')), may hold values from -1 to 0
- token_codes: int32 [32768], P(('ctx', 'head')), may hold values from 0 to 63
- level_table: bfloat16 [64, 1408], replicated, may hold values from 0.099609375 to 1
- skip_gain: float32 [128], replicated, may hold values from 0.2 to 1
Outputs:
- mixed_output: bfloat16 [32768, 8192], P(('ctx', 'head'))
All inputs are finite; a program needn't handle non-finite values.
Results may differ from a plain program's by a relative error of at most 0.009.
Values may be sent and summed in bfloat16 or wider, within the bound.
A program may use at most 64 MiB of HBM per device.

v0:
```python
import jax
import jax.numpy as jnp
from jax import lax
from jax.sharding import PartitionSpec as P

COUNT_OF_HEADS = 128
HEAD_DIM = 64
SPAN = 64
LEVELS = 11


def swapped(x, axis, apart):
    return lax.ppermute(x, axis, [(i, i ^ 1 << apart) for i in range(lax.axis_size(axis))])


def look_up(token_codes, weight_table):
    one_hot = (
        token_codes[:, None] == jnp.arange(weight_table.shape[0], dtype=jnp.int32)[None, :]
    ).astype(jnp.bfloat16)
    return jnp.dot(one_hot, weight_table, preferred_element_type=jnp.float32).astype(jnp.bfloat16)


def level_onehot(spans, levels):
    span_ids = jnp.arange(spans, dtype=jnp.int32)
    xored = jnp.bitwise_xor(span_ids[:, None], span_ids[None, :])
    level_ids = jnp.zeros((spans, spans), jnp.int32)
    for level_bit in range(max(spans.bit_length() - 1, 0)):
        level_ids = level_ids + (xored >= 1 << level_bit).astype(jnp.int32)
    return (level_ids[:, :, None] == jnp.arange(levels, dtype=jnp.int32)[None, None, :]).astype(
        jnp.float32
    )


def head_local(scores, head_input, head_weights, head_running, onehot, span):
    block_rows = head_input.shape[0]
    spans = block_rows // span
    weight_blocks = head_weights.astype(jnp.float32).reshape(spans, span, -1)
    pair_weights = jnp.einsum(
        "iql,ijl->iqj", weight_blocks, onehot, precision=lax.Precision.HIGHEST
    )
    row_weights = jnp.broadcast_to(
        pair_weights.reshape(block_rows, spans, 1), (block_rows, spans, span)
    ).reshape(block_rows, block_rows)
    position = jnp.arange(block_rows)
    causal = position[:, None] >= position[None, :]
    log_gap = jnp.where(causal, head_running[:, None] - head_running[None, :], 0.0)
    decay_factor = jnp.where(causal, jnp.exp(log_gap), 0.0)
    weight = (row_weights * decay_factor * scores).astype(jnp.bfloat16)
    return jnp.dot(weight, head_input, preferred_element_type=jnp.float32)


def head_state(head_input, head_running, state_in):
    carried = jnp.exp(head_running[-1] - head_running)[:, None] * head_input.astype(jnp.float32)
    return jnp.einsum(
        "tn,tp->np", state_in, carried.astype(jnp.bfloat16), preferred_element_type=jnp.float32
    )


def finish(
    local_part,
    head_input,
    head_weights,
    head_running,
    state_out,
    bucket_states,
    skip_value,
    span_bits,
    ctx_bits,
):
    reached = jnp.einsum(
        "tn,mnp->tmp", state_out, bucket_states, preferred_element_type=jnp.float32
    )
    factors = (
        head_weights[:, span_bits + 1 : span_bits + 1 + ctx_bits].astype(jnp.float32)
        * jnp.exp(head_running)[:, None]
    )
    cross_part = jnp.sum(factors[:, :, None] * reached, axis=1)
    return (local_part + cross_part + skip_value * head_input.astype(jnp.float32)).astype(
        jnp.bfloat16
    )


def on_device(token_inputs, state_in, state_out, log_decay, token_codes, level_table, skip_gain):
    head_ways = lax.axis_size("head")
    local_heads = COUNT_OF_HEADS // head_ways
    offset = lax.axis_index("head")
    weights_seq = look_up(token_codes, level_table)
    moved_rows, moved_weights, moved_decay = (
        lax.all_to_all(token_inputs, "head", split_axis=1, concat_axis=0, tiled=True),
        lax.all_to_all(weights_seq, "head", split_axis=1, concat_axis=0, tiled=True),
        lax.all_to_all(log_decay, "head", split_axis=1, concat_axis=0, tiled=True),
    )
    in_all, out_all = (
        lax.all_gather(state_in, "head", axis=0, tiled=True),
        lax.all_gather(state_out, "head", axis=0, tiled=True),
    )
    block_rows = moved_rows.shape[0]
    spans = block_rows // SPAN
    span_bits = spans.bit_length() - 1
    input_all = moved_rows.reshape(block_rows, local_heads, HEAD_DIM)
    weights_all = moved_weights.reshape(block_rows, local_heads, LEVELS)
    running = jnp.cumsum(moved_decay.astype(jnp.float32), axis=0)
    onehot = level_onehot(spans, LEVELS)
    scores = jnp.einsum("tn,sn->ts", out_all, in_all, preferred_element_type=jnp.float32)

    def first_pass(head_index):
        head_input = input_all[:, head_index]
        head_running = running[:, head_index]
        local_part = head_local(
            scores, head_input, weights_all[:, head_index], head_running, onehot, SPAN
        )
        return (local_part, head_state(head_input, head_running, in_all))

    local_all, states = lax.map(first_pass, jnp.arange(local_heads))
    summary = states
    summary_decay = running[-1]
    inside = jnp.zeros_like(summary_decay)
    device = lax.axis_index("ctx")
    ctx_bits = lax.axis_size("ctx").bit_length() - 1
    buckets = []
    for level_bit in range(ctx_bits):
        partner, partner_decay = (
            swapped(summary.astype(jnp.bfloat16), "ctx", level_bit).astype(summary.dtype),
            swapped(summary_decay.astype(jnp.bfloat16), "ctx", level_bit).astype(
                summary_decay.dtype
            ),
        )
        is_upper = device >> level_bit & 1 == 1
        buckets.append(
            jnp.where(is_upper, partner * jnp.exp(inside)[:, None, None], 0.0).astype(jnp.bfloat16)
        )
        summary = jnp.where(
            is_upper,
            partner * jnp.exp(summary_decay)[:, None, None] + summary,
            summary * jnp.exp(partner_decay)[:, None, None] + partner,
        )
        inside = jnp.where(is_upper, inside + partner_decay, inside)
        summary_decay = summary_decay + partner_decay
    bucket_stack = jnp.stack(buckets, axis=0)
    gains = lax.dynamic_slice_in_dim(skip_gain, offset * local_heads, local_heads, 0)

    def second_pass(head_index):
        return finish(
            local_all[head_index],
            input_all[:, head_index],
            weights_all[:, head_index],
            running[:, head_index],
            out_all,
            bucket_stack[:, head_index],
            gains[head_index],
            span_bits,
            ctx_bits,
        )

    mixed_rows = lax.map(second_pass, jnp.arange(local_heads))
    merged = jnp.moveaxis(mixed_rows, 0, 1).reshape(block_rows, local_heads * HEAD_DIM)
    return lax.all_to_all(merged, "head", split_axis=0, concat_axis=1, tiled=True)


def solution(mesh):
    return jax.shard_map(
        on_device,
        mesh=mesh,
        in_specs=(
            P(("ctx", "head"), None),
            P(("ctx", "head"), None),
            P(("ctx", "head"), None),
            P(("ctx", "head"), None),
            P(("ctx", "head")),
            P(),
            P(),
        ),
        out_specs=P(("ctx", "head"), None),
        check_vma=False,
    )
```

profile of v0, /device:TPU:1, one launch (start us, length us, event | category | flops | bytes accessed | tf_op | source)
XLA Modules:
  0.0 465.8 jit_solution(6821224827247671395)
XLA Ops:
  1.6 10.1 %all-to-all-start.1 = ((bf16[8,2,512]{2,1,0:T(2,128)(2,1)}), bf16[8,2,512]{2,1,0:T(2,128)(2,1)S(1)}, u32[]{:S(2)}, u32[]{:S(2)}) async-start(bf16[8,2,512]{2,1,0:T(2,128)(2,1)} %reshape.216), calls=%async_computation.1 | async-start | bytes 32768 | tf_op jit(solution)/shard_map/all_to_all | solution.py:91
  11.7 13.7 %all_gather.6 = bf16[512,128]{1,0:T(8,128)(2,1)S(1)} all-gather(bf16[64,128]{1,0:T(8,128)(2,1)} %param.13), channel_id=1, replica_groups=mesh['ctx'=64,'head'=8] {'head'}, dimensions={0}, use_global_device_ids=true | all-gather | bytes 147456 | tf_op jit(solution)/shard_map/all_gather | solution.py:95
  25.4 12.9 %all_gather.7 = bf16[512,128]{1,0:T(8,128)(2,1)S(1)} all-gather(bf16[64,128]{1,0:T(8,128)(2,1)} %param.12), channel_id=1, replica_groups=mesh['ctx'=64,'head'=8] {'head'}, dimensions={0}, use_global_device_ids=true | all-gather | bytes 147456 | tf_op jit(solution)/shard_map/all_gather | solution.py:94
  41.2 3.8 all-to-all-start
  46.6 4.9 %all-to-all-done = bf16[64,8,176]{2,0,1:T(8,128)(2,1)S(1)} async-done(((bf16[64,8,176]{2,0,1:T(8,128)(2,1)}), bf16[64,8,176]{2,0,1:T(8,128)(2,1)S(1)}, u32[]{:S(2)}, u32[]{:S(2)}) %all-to-all-start) | async-done | bytes 180256 | tf_op jit(solution)/shard_map/all_to_all | solution.py:90
  51.5 4.5 all-to-all-start.2
  58.2 2.7 collective-permute-done.1
  62.8 3.6 collective-permute-done.3
  66.4 3.1 collective-permute-start.5
  69.5 5.1 %collective-permute-done.5 = bf16[16]{0:T(256)(128)(2,1)S(1)} collective-permute-done((bf16[16]{0:T(256)(128)(2,1)S(1)}, bf16[16]{0:T(256)(128)(2,1)S(1)}, u32[]{:S(2)}, u32[]{:S(2)}) %collective-permute-start.5) | collective-permute-done | bytes 64 | tf_op jit(solution)/shard_map/ppermute | solution.py:13
  78.7 2.9 reshape.198
  84.2 159.0 %while.26 = (s32[]{:T(128)}, f32[16,512,64]{1,2,0:T(8,128)}, f32[16,128,64]{1,2,0:T(8,128)}, s32[16]{0:T(128)S(1)}, bf16[512,16,11]{0,2,1:T(8,128)(2,1)}, /*inde...) while((s32[]{:T(128)}, f32[16,512,64]{1,2,0:T(8,128)}, ...), condition=%wide.region_3.4_spmd.clone.clone, body=%wide.region_2.3_spmd.clone.sunk.clone | while | flops 44419972 | bytes 2703819 | solution.py:114
  246.3 4.9 %collective-permute-start.9 = (bf16[16]{0:T(256)(128)(2,1)S(1)}, bf16[16]{0:T(256)(128)(2,1)S(1)}, u32[]{:S(2)}, u32[]{:S(2)}) collective-permute-start(bf16[16]{0:T(256)(128)(2,1)S(1)} %get-tuple-element.258), channel_id=1, source_target_pairs={{0,128},{8,136},{16,144},{24,152},{32,160},{40,168},{48,176},{56,1... | collective-permute-start | bytes 104 | tf_op jit(solution)/shard_map/ppermute | solution.py:13
  253.4 4.2 collective-permute-start.2
  257.6 10.5 %collective-permute-done.2 = bf16[16,128,64]{1,2,0:T(8,128)(2,1)S(1)} collective-permute-done((bf16[16,128,64]{1,2,0:T(8,128)(2,1)S(1)}, bf16[16,128,64]{1,2,0:T(8,128)(2,1)S(1)}, u32[]{:S(2)}, u32[]{:S(2)}) %collective-permute-start.2) | collective-permute-done | bytes 262176 | tf_op jit(solution)/shard_map/ppermute | solution.py:13
  268.4 6.6 %collective-permute-start.4 = (bf16[16,128,64]{1,2,0:T(8,128)(2,1)S(1)}, bf16[16,128,64]{1,2,0:T(8,128)(2,1)S(1)}, u32[]{:S(2)}, u32[]{:S(2)}) collective-permute-start(bf16[16,128,64]{1,2,0:T(8,128)(2,1)S(1)} %fusion.67), channel_id=1, source_target_pairs={{0,32},{8,40},{16,48},{24,56},{32,0},{40,8},{48,16},{56,24},{64,96... | collective-permute-start | bytes 786440 | tf_op jit(solution)/shard_map/ppermute | solution.py:13
  275.1 11.6 %collective-permute-done.4 = bf16[16,128,64]{1,2,0:T(8,128)(2,1)S(1)} collective-permute-done((bf16[16,128,64]{1,2,0:T(8,128)(2,1)S(1)}, bf16[16,128,64]{1,2,0:T(8,128)(2,1)S(1)}, u32[]{:S(2)}, u32[]{:S(2)}) %collective-permute-start.4) | collective-permute-done | bytes 262176 | tf_op jit(solution)/shard_map/ppermute | solution.py:13
  289.1 5.8 %collective-permute-done.6 = bf16[16,128,64]{1,2,0:T(8,128)(2,1)S(1)} collective-permute-done((bf16[16,128,64]{1,2,0:T(8,128)(2,1)S(1)}, bf16[16,128,64]{1,2,0:T(8,128)(2,1)S(1)}, u32[]{:S(2)}, u32[]{:S(2)}) %collective-permute-start.6) | collective-permute-done | bytes 262176 | tf_op jit(solution)/shard_map/ppermute | solution.py:13
  295.1 3.1 collective-permute-start.8
  298.6 13.1 %collective-permute-done.8 = bf16[16,128,64]{1,2,0:T(8,128)(2,1)S(1)} collective-permute-done((bf16[16,128,64]{1,2,0:T(8,128)(2,1)S(1)}, bf16[16,128,64]{1,2,0:T(8,128)(2,1)S(1)}, u32[]{:S(2)}, u32[]{:S(2)}) %collective-permute-start.8) | collective-permute-done | bytes 262176 | tf_op jit(solution)/shard_map/ppermute | solution.py:13
  312.0 4.5 collective-permute-start.10
  316.9 14.3 %collective-permute-done.10 = bf16[16,128,64]{1,2,0:T(8,128)(2,1)S(1)} collective-permute-done((bf16[16,128,64]{1,2,0:T(8,128)(2,1)S(1)}, bf16[16,128,64]{1,2,0:T(8,128)(2,1)S(1)}, u32[]{:S(2)}, u32[]{:S(2)}) %collective-permute-start.10) | collective-permute-done | bytes 262176 | tf_op jit(solution)/shard_map/ppermute | solution.py:13
  332.5 111.8 %while.25 = (s32[]{:T(128)}, bf16[16,512,64]{1,2,0:T(8,128)(2,1)S(1)}, s32[16]{0:T(128)S(1)}, f32[16,512,64]{1,2,0:T(8,128)}, bf16[512,16,11]{0,2,1:T(8,128)(2,1...) while((s32[]{:T(128)}, ...), condition=%wide.region_6.7_spmd.clone, body=%wide.region_4.6_spmd.sunk.clone | while | flops 50862084 | bytes 813239 | solution.py:155
  446.9 17.8 %all_to_all.64 = bf16[8,64,1024]{2,1,0:T(8,128)(2,1)S(1)} all-to-all(bf16[8,64,1024]{2,1,0:T(8,128)(2,1)S(1)} %copy.58), channel_id=1, replica_groups=mesh['ctx'=64,'head'=8] {'head'}, dimensions={0} | all-to-all | bytes 2097152 | tf_op jit(solution)/shard_map/all_to_all | solution.py:157
  (433 shorter events, 237.5 us)
Async XLA Ops:
  0.0 38.6 %copy-start = (bf16[64,1408]{1,0:T(8,128)(2,1)S(1)}, bf16[64,1408]{1,0:T(8,128)(2,1)}, u32[]{:S(2)}) copy-start(bf16[64,1408]{1,0:T(8,128)(2,1)} %param.16) | copy-start | bytes 540676
  0.0 38.6 %copy-start.7 = (s32[64]{0:T(128)S(1)}, s32[64]{0:T(128)}, u32[]{:S(2)}) copy-start(s32[64]{0:T(128)} %param.15) | copy-start | bytes 772
  0.0 38.9 %copy-start.3 = (bf16[64,8192]{1,0:T(8,128)(2,1)S(1)}, bf16[64,8192]{1,0:T(8,128)(2,1)}, u32[]{:S(2)}) copy-start(bf16[64,8192]{1,0:T(8,128)(2,1)} %param.11) | copy-start | bytes 3145732
  1.6 39.5 %all-to-all-start.1 = ((bf16[8,2,512]{2,1,0:T(2,128)(2,1)}), bf16[8,2,512]{2,1,0:T(2,128)(2,1)S(1)}, u32[]{:S(2)}, u32[]{:S(2)}) async-start(bf16[8,2,512]{2,1,0:T(2,128)(2,1)} %reshape.216), calls=%async_computation.1 | async-start | bytes 32768 | tf_op jit(solution)/shard_map/all_to_all | solution.py:91
  25.4 13.0 %copy-start.4 = (bf16[512,128]{1,0:T(8,128)(2,1)}, bf16[512,128]{1,0:T(8,128)(2,1)S(1)}, u32[]{:S(2)}) copy-start(bf16[512,128]{1,0:T(8,128)(2,1)S(1)} %all_gather.6) | copy-start | bytes 393220
  41.2 10.3 %all-to-all-start = ((bf16[64,8,176]{2,0,1:T(8,128)(2,1)}), bf16[64,8,176]{2,0,1:T(8,128)(2,1)S(1)}, u32[]{:S(2)}, u32[]{:S(2)}) async-start(bf16[64,8,176]{2,0,1:T(8,128)(2,1)} %copy.44), calls=%async_computation | async-start | bytes 524288 | tf_op jit(solution)/shard_map/all_to_all | solution.py:90
  51.5 26.3 %all-to-all-start.2 = ((bf16[64,8,1024]{2,0,1:T(8,128)(2,1)}), bf16[64,8,1024]{2,0,1:T(8,128)(2,1)S(1)}, u32[]{:S(2)}, u32[]{:S(2)}) async-start(bf16[64,8,1024]{2,0,1:T(8,128)(2,1)} %bitcast.122), calls=%async_computation.2 | async-start | bytes 2097152 | tf_op jit(solution)/shard_map/all_to_all | solution.py:89
  56.2 4.6 collective-permute-start.1
  60.9 5.5 %collective-permute-start.3 = (bf16[16]{0:T(256)(128)(2,1)S(1)}, bf16[16]{0:T(256)(128)(2,1)S(1)}, u32[]{:S(2)}, u32[]{:S(2)}) collective-permute-start(bf16[16]{0:T(256)(128)(2,1)S(1)} %fusion.63), channel_id=1, source_target_pairs={{0,16},{8,24},{16,0},{24,8},{32,48},{40,56},{48,32},{56,40},{64,80... | collective-permute-start | bytes 104 | tf_op jit(solution)/shard_map/ppermute | solution.py:13
  66.4 8.2 %collective-permute-start.5 = (bf16[16]{0:T(256)(128)(2,1)S(1)}, bf16[16]{0:T(256)(128)(2,1)S(1)}, u32[]{:S(2)}, u32[]{:S(2)}) collective-permute-start(bf16[16]{0:T(256)(128)(2,1)S(1)} %convert_element_type.176), channel_id=1, source_target_pairs={{0,32},{8,40},{16,48},{24,56},{32,0},{40,8},{48,16},{56,24},{64,96... | collective-permute-start | bytes 104 | tf_op jit(solution)/shard_map/ppermute | solution.py:13
  74.6 171.7 %collective-permute-start.7 = (bf16[16]{0:T(256)(128)(2,1)S(1)}, bf16[16]{0:T(256)(128)(2,1)S(1)}, u32[]{:S(2)}, u32[]{:S(2)}) collective-permute-start(bf16[16]{0:T(256)(128)(2,1)S(1)} %convert_element_type.181), channel_id=1, source_target_pairs={{0,64},{8,72},{16,80},{24,88},{32,96},{40,104},{48,112},{56,120},{... | collective-permute-start | bytes 104 | tf_op jit(solution)/shard_map/ppermute | solution.py:13
  77.8 1.0 copy-start.2
  243.2 24.9 %copy-start.1 = (f32[16,128,64]{1,2,0:T(8,128)S(1)}, f32[16,128,64]{1,2,0:T(8,128)}, u32[]{:S(2)}) copy-start(f32[16,128,64]{1,2,0:T(8,128)} %get-tuple-element.111) | copy-start | bytes 1572868
  243.2 31.8 %copy-start.8 = (f32[128]{0:T(128)S(1)}, f32[128]{0:T(128)}, u32[]{:S(2)}) copy-start(f32[128]{0:T(128)} %param.17) | copy-start | bytes 1540
  244.3 7.8 %collective-permute-start = (bf16[16,128,64]{1,2,0:T(8,128)(2,1)S(1)}, bf16[16,128,64]{1,2,0:T(8,128)(2,1)S(1)}, u32[]{:S(2)}, u32[]{:S(2)}) collective-permute-start(bf16[16,128,64]{1,2,0:T(8,128)(2,1)S(1)} %convert_element_type.163), channel_id=1, source_target_pairs={{0,8},{8,0},{16,24},{24,16},{32,40},{40,32},{48,56},{56,48},{64,72... | collective-permute-start | bytes 786440 | tf_op jit(solution)/shard_map/ppermute | solution.py:13
  246.3 5.8 %collective-permute-start.9 = (bf16[16]{0:T(256)(128)(2,1)S(1)}, bf16[16]{0:T(256)(128)(2,1)S(1)}, u32[]{:S(2)}, u32[]{:S(2)}) collective-permute-start(bf16[16]{0:T(256)(128)(2,1)S(1)} %get-tuple-element.258), channel_id=1, source_target_pairs={{0,128},{8,136},{16,144},{24,152},{32,160},{40,168},{48,176},{56,1... | collective-permute-start | bytes 104 | tf_op jit(solution)/shard_map/ppermute | solution.py:13
  253.4 14.7 %collective-permute-start.2 = (bf16[16,128,64]{1,2,0:T(8,128)(2,1)S(1)}, bf16[16,128,64]{1,2,0:T(8,128)(2,1)S(1)}, u32[]{:S(2)}, u32[]{:S(2)}) collective-permute-start(bf16[16,128,64]{1,2,0:T(8,128)(2,1)S(1)} %fusion.68), channel_id=1, source_target_pairs={{0,16},{8,24},{16,0},{24,8},{32,48},{40,56},{48,32},{56,40},{64,80... | collective-permute-start | bytes 786440 | tf_op jit(solution)/shard_map/ppermute | solution.py:13
  268.4 18.2 %collective-permute-start.4 = (bf16[16,128,64]{1,2,0:T(8,128)(2,1)S(1)}, bf16[16,128,64]{1,2,0:T(8,128)(2,1)S(1)}, u32[]{:S(2)}, u32[]{:S(2)}) collective-permute-start(bf16[16,128,64]{1,2,0:T(8,128)(2,1)S(1)} %fusion.67), channel_id=1, source_target_pairs={{0,32},{8,40},{16,48},{24,56},{32,0},{40,8},{48,16},{56,24},{64,96... | collective-permute-start | bytes 786440 | tf_op jit(solution)/shard_map/ppermute | solution.py:13
  287.1 7.9 %collective-permute-start.6 = (bf16[16,128,64]{1,2,0:T(8,128)(2,1)S(1)}, bf16[16,128,64]{1,2,0:T(8,128)(2,1)S(1)}, u32[]{:S(2)}, u32[]{:S(2)}) collective-permute-start(bf16[16,128,64]{1,2,0:T(8,128)(2,1)S(1)} %get-tuple-element.253), channel_id=1, source_target_pairs={{0,64},{8,72},{16,80},{24,88},{32,96},{40,104},{48,112},{56,120},{... | collective-permute-start | bytes 786440 | tf_op jit(solution)/shard_map/ppermute | solution.py:13
  295.1 16.6 %collective-permute-start.8 = (bf16[16,128,64]{1,2,0:T(8,128)(2,1)S(1)}, bf16[16,128,64]{1,2,0:T(8,128)(2,1)S(1)}, u32[]{:S(2)}, u32[]{:S(2)}) collective-permute-start(bf16[16,128,64]{1,2,0:T(8,128)(2,1)S(1)} %fusion.66), channel_id=1, source_target_pairs={{0,128},{8,136},{16,144},{24,152},{32,160},{40,168},{48,176},{56,1... | collective-permute-start | bytes 786440 | tf_op jit(solution)/shard_map/ppermute | solution.py:13
  298.6 33.9 %copy-start.5 = (bf16[512,128]{1,0:T(8,128)(2,1)S(1)}, bf16[512,128]{1,0:T(8,128)(2,1)}, u32[]{:S(2)}) copy-start(bf16[512,128]{1,0:T(8,128)(2,1)} %copy-done.4) | copy-start | bytes 393220
  312.0 19.1 %collective-permute-start.10 = (bf16[16,128,64]{1,2,0:T(8,128)(2,1)S(1)}, bf16[16,128,64]{1,2,0:T(8,128)(2,1)S(1)}, u32[]{:S(2)}, u32[]{:S(2)}) collective-permute-start(bf16[16,128,64]{1,2,0:T(8,128)(2,1)S(1)} %fusion.42), channel_id=1, source_target_pairs={{0,256},{8,264},{16,272},{24,280},{32,288},{40,296},{48,304},{56,3... | collective-permute-start | bytes 786440 | tf_op jit(solution)/shard_map/ppermute | solution.py:13
  331.4 1.2 copy-start.6
where the time goes:
time: 472 us; the launch traced here: 466 us
  local copies, waits for them, and re-layouts  95.3 us (20%)
  matrix products  75.6 us (16%)
  waiting for transfers between devices  72.5 us (15%)
  loops' own time  64.2 us (14%)
  other arithmetic  59 us (12%)
  starting transfers between devices  54.4 us (12%)
  blocking collectives  44.4 us (9%)
    ppermute x11, waiting for transfers between devices, swapped(): lax.ppermute(x, axis, [(i, i ^ 1 << apart) for i in range(lax.axis_size(a...  67.5 us
    ppermute x11, starting transfers between devices, swapped(): lax.ppermute(x, axis, [(i, i ^ 1 << apart) for i in range(lax.axis_size(a...  36 us
    another operation x1, loops' own time, on_device(): mixed_rows = lax.map(second_pass, jnp.arange(local_heads))  33.8 us
    another operation x1, loops' own time, on_device(): local_all, states = lax.map(first_pass, jnp.arange(local_heads))  30.4 us
    dot_general x16, matrix products, head_local(): return jnp.dot(weight, head_input, preferred_element_type=jnp.float32)  27.3 us
    dynamic_update_slice x16, other arithmetic, on_device(): mixed_rows = lax.map(second_pass, jnp.arange(local_heads))  26 us
    dot_general x16, matrix products, head_state(): jnp.einsum('tn,tp->np', state_in, carried.astype(jnp.bfloat16), preferred...  25.6 us
    dynamic_slice x32, local copies, waits for them, and re-layouts, on_device(): local_all, states = lax.map(first_pass, jnp.arange(local_heads))  20.8 us
  transfers between devices with their start and end apart: 14, of which 10 were waited for; matrix products, arithmetic and copies ran while one was open for 30% of the time, Pallas kernels for 0%

commit v1 on v0

--- a/solution.py
+++ b/solution.py
@@ -2,6 +2,7 @@
 import jax.numpy as jnp
 from jax import lax
 from jax.sharding import PartitionSpec as P
+from jax.lax import all_to_all, axis_size
 
 COUNT_OF_HEADS = 128
 HEAD_DIM = 64
@@ -90,8 +91,15 @@
         lax.all_to_all(weights_seq, "head", split_axis=1, concat_axis=0, tiled=True),
         lax.all_to_all(log_decay, "head", split_axis=1, concat_axis=0, tiled=True),
     )
+
+    def extend_the_rows(body):
+        r_now = jnp.concatenate(
+            all_to_all(jnp.stack(axis_size("head") * [body], axis=0), "head", 0, 0), axis=0
+        )
+        return r_now
+
     in_all, out_all = (
-        lax.all_gather(state_in, "head", axis=0, tiled=True),
+        extend_the_rows(state_in),
         lax.all_gather(state_out, "head", axis=0, tiled=True),
     )
     block_rows = moved_rows.shape[0]

time: 472 us -> 458 us (0.970)
  starting transfers between devices: 54.4 us -> 65 us
  waiting for transfers between devices: 72.5 us -> 63.9 us
  blocking collectives: 44.4 us -> 36.9 us
  loops' own time: 64.2 us -> 58.8 us
    all_gather x1 -> x0, blocking collectives: 12.9 us -> none  [on_device(): lax.all_gather(state_in, 'head', axis=0, tiled=True)]
    ppermute x11, waiting for transfers between devices: 67.5 us -> 55.9 us  [swapped(): lax.ppermute(x, axis, [(i, i ^ 1 << apart) for i in range(lax.axis_size(a...]
    ppermute x11, starting transfers between devices: 36 us -> 42.4 us  [swapped(): lax.ppermute(x, axis, [(i, i ^ 1 << apart) for i in range(lax.axis_size(a...]
    another operation x1, loops' own time: 33.8 us -> 27.9 us  [on_device(): mixed_rows = lax.map(second_pass, jnp.arange(local_heads))]
    all_to_all x1, blocking collectives: 17.8 us -> 23.2 us  [on_device(): lax.all_to_all(merged, 'head', split_axis=0, concat_axis=1, tiled=True)]
  transfers between devices with their start and end apart: 14 -> 15, of which waited for: 10 -> 10; matrix products, arithmetic and copies ran while one was open for 30% -> 31% of each run, Pallas kernels for 0% -> 0%
where the time goes in v1:
time: 458 us; the launch traced here: 451 us
  local copies, waits for them, and re-layouts  92.6 us (20%)
  matrix products  76.4 us (17%)
  starting transfers between devices  65 us (14%)
  waiting for transfers between devices  63.9 us (14%)
  loops' own time  58.8 us (13%)
  other arithmetic  57.4 us (13%)
  blocking collectives  36.9 us (8%)
    ppermute x11, waiting for transfers between devices, swapped(): lax.ppermute(x, axis, [(i, i ^ 1 << apart) for i in range(lax.axis_size(a...  55.9 us
    ppermute x11, starting transfers between devices, swapped(): lax.ppermute(x, axis, [(i, i ^ 1 << apart) for i in range(lax.axis_size(a...  42.4 us
    another operation x1, loops' own time, on_device(): local_all, states = lax.map(first_pass, jnp.arange(local_heads))  31 us
    another operation x1, loops' own time, on_device(): mixed_rows = lax.map(second_pass, jnp.arange(local_heads))  27.9 us
    dot_general x16, matrix products, head_local(): return jnp.dot(weight, head_input, preferred_element_type=jnp.float32)  27.3 us
    dot_general x16, matrix products, head_state(): jnp.einsum('tn,tp->np', state_in, carried.astype(jnp.bfloat16), preferred...  25.7 us
    dynamic_update_slice x16, other arithmetic, on_device(): mixed_rows = lax.map(second_pass, jnp.arange(local_heads))  24 us
    all_to_all x1, blocking collectives, on_device(): lax.all_to_all(merged, 'head', split_axis=0, concat_axis=1, tiled=True)  23.2 us
  transfers between devices with their start and end apart: 15, of which 10 were waited for; matrix products, arithmetic and copies ran while one was open for 31% of the time, Pallas kernels for 0%

profile of v1, /device:TPU:1, one launch (start us, length us, event | category | flops | bytes accessed | tf_op | source)
XLA Modules:
  0.0 451.3 jit_solution(16849872323951206448)
XLA Ops:
  1.6 10.1 %all-to-all-start.1 = ((bf16[8,2,512]{2,1,0:T(2,128)(2,1)}), bf16[8,2,512]{2,1,0:T(2,128)(2,1)S(1)}, u32[]{:S(2)}, u32[]{:S(2)}) async-start(bf16[8,2,512]{2,1,0:T(2,128)(2,1)} %reshape.222), calls=%async_computation.1 | async-start | bytes 32768 | tf_op jit(solution)/shard_map/all_to_all | solution.py:92
  12.6 13.7 %all_gather.3 = bf16[512,128]{1,0:T(8,128)(2,1)S(1)} all-gather(bf16[64,128]{1,0:T(8,128)(2,1)} %param.13), channel_id=1, replica_groups=mesh['ctx'=64,'head'=8] {'head'}, dimensions={0}, use_global_device_ids=true | all-gather | bytes 147456 | tf_op jit(solution)/shard_map/all_gather | solution.py:103
  30.4 3.8 all-to-all-start.2
  35.8 3.7 all-to-all-done.2
  39.5 4.2 all-to-all-start
  45.9 4.3 all-to-all-done
  50.2 4.5 all-to-all-start.3
  56.6 3.6 collective-permute-done.3
  60.2 3.1 collective-permute-start.5
  63.4 5.1 %collective-permute-done.5 = bf16[16]{0:T(256)(128)(2,1)S(1)} collective-permute-done((bf16[16]{0:T(256)(128)(2,1)S(1)}, bf16[16]{0:T(256)(128)(2,1)S(1)}, u32[]{:S(2)}, u32[]{:S(2)}) %collective-permute-start.5) | collective-permute-done | bytes 64 | tf_op jit(solution)/shard_map/ppermute | solution.py:14
  78.3 158.3 %while.26 = (s32[]{:T(128)}, f32[16,512,64]{1,2,0:T(8,128)}, f32[16,128,64]{1,2,0:T(8,128)}, s32[16]{0:T(128)S(1)}, bf16[512,16,11]{0,2,1:T(8,128)(2,1)}, /*inde...) while((s32[]{:T(128)}, f32[16,512,64]{1,2,0:T(8,128)}, ...), condition=%wide.region_3.4_spmd.clone.clone, body=%wide.region_2.3_spmd.clone.sunk.clone | while | flops 44419972 | bytes 2703819 | solution.py:122
  239.8 4.9 %collective-permute-start.9 = (bf16[16]{0:T(256)(128)(2,1)S(1)}, bf16[16]{0:T(256)(128)(2,1)S(1)}, u32[]{:S(2)}, u32[]{:S(2)}) collective-permute-start(bf16[16]{0:T(256)(128)(2,1)S(1)} %get-tuple-element.258), channel_id=1, source_target_pairs={{0,128},{8,136},{16,144},{24,152},{32,160},{40,168},{48,176},{56,1... | collective-permute-start | bytes 104 | tf_op jit(solution)/shard_map/ppermute | solution.py:14
  246.9 4.2 collective-permute-start.2
  251.1 11.3 %collective-permute-done.2 = bf16[16,128,64]{1,2,0:T(8,128)(2,1)S(1)} collective-permute-done((bf16[16,128,64]{1,2,0:T(8,128)(2,1)S(1)}, bf16[16,128,64]{1,2,0:T(8,128)(2,1)S(1)}, u32[]{:S(2)}, u32[]{:S(2)}) %collective-permute-start.2) | collective-permute-done | bytes 262176 | tf_op jit(solution)/shard_map/ppermute | solution.py:14
  262.7 6.5 %collective-permute-start.4 = (bf16[16,128,64]{1,2,0:T(8,128)(2,1)S(1)}, bf16[16,128,64]{1,2,0:T(8,128)(2,1)S(1)}, u32[]{:S(2)}, u32[]{:S(2)}) collective-permute-start(bf16[16,128,64]{1,2,0:T(8,128)(2,1)S(1)} %fusion.67), channel_id=1, source_target_pairs={{0,32},{8,40},{16,48},{24,56},{32,0},{40,8},{48,16},{56,24},{64,96... | collective-permute-start | bytes 786440 | tf_op jit(solution)/shard_map/ppermute | solution.py:14
  269.4 11.5 %collective-permute-done.4 = bf16[16,128,64]{1,2,0:T(8,128)(2,1)S(1)} collective-permute-done((bf16[16,128,64]{1,2,0:T(8,128)(2,1)S(1)}, bf16[16,128,64]{1,2,0:T(8,128)(2,1)S(1)}, u32[]{:S(2)}, u32[]{:S(2)}) %collective-permute-start.4) | collective-permute-done | bytes 262176 | tf_op jit(solution)/shard_map/ppermute | solution.py:14
  281.3 3.2 collective-permute-start.6
  284.6 4.4 collective-permute-done.6
  289.2 4.0 collective-permute-start.8
  293.6 10.8 %collective-permute-done.8 = bf16[16,128,64]{1,2,0:T(8,128)(2,1)S(1)} collective-permute-done((bf16[16,128,64]{1,2,0:T(8,128)(2,1)S(1)}, bf16[16,128,64]{1,2,0:T(8,128)(2,1)S(1)}, u32[]{:S(2)}, u32[]{:S(2)}) %collective-permute-start.8) | collective-permute-done | bytes 262176 | tf_op jit(solution)/shard_map/ppermute | solution.py:14
  304.7 8.8 %collective-permute-start.10 = (bf16[16,128,64]{1,2,0:T(8,128)(2,1)S(1)}, bf16[16,128,64]{1,2,0:T(8,128)(2,1)S(1)}, u32[]{:S(2)}, u32[]{:S(2)}) collective-permute-start(bf16[16,128,64]{1,2,0:T(8,128)(2,1)S(1)} %fusion.42), channel_id=1, source_target_pairs={{0,256},{8,264},{16,272},{24,280},{32,288},{40,296},{48,304},{56,3... | collective-permute-start | bytes 786440 | tf_op jit(solution)/shard_map/ppermute | solution.py:14
  313.9 8.2 %collective-permute-done.10 = bf16[16,128,64]{1,2,0:T(8,128)(2,1)S(1)} collective-permute-done((bf16[16,128,64]{1,2,0:T(8,128)(2,1)S(1)}, bf16[16,128,64]{1,2,0:T(8,128)(2,1)S(1)}, u32[]{:S(2)}, u32[]{:S(2)}) %collective-permute-start.10) | collective-permute-done | bytes 262176 | tf_op jit(solution)/shard_map/ppermute | solution.py:14
  323.4 101.0 %while.25 = (s32[]{:T(128)}, bf16[16,512,64]{1,2,0:T(8,128)(2,1)S(1)}, s32[16]{0:T(128)S(1)}, f32[16,512,64]{1,2,0:T(8,128)}, bf16[512,16,11]{0,2,1:T(8,128)(2,1...) while((s32[]{:T(128)}, ...), condition=%wide.region_6.7_spmd.clone, body=%wide.region_4.6_spmd.sunk.clone | while | flops 50862084 | bytes 813239 | solution.py:163
  427.1 23.2 %all_to_all.69 = bf16[8,64,1024]{2,1,0:T(8,128)(2,1)S(1)} all-to-all(bf16[8,64,1024]{2,1,0:T(8,128)(2,1)S(1)} %copy.58), channel_id=1, replica_groups=mesh['ctx'=64,'head'=8] {'head'}, dimensions={0} | all-to-all | bytes 2097152 | tf_op jit(solution)/shard_map/all_to_all | solution.py:165
  (433 shorter events, 235.0 us)
Async XLA Ops:
  0.0 11.7 %copy-start = (bf16[64,1408]{1,0:T(8,128)(2,1)S(1)}, bf16[64,1408]{1,0:T(8,128)(2,1)}, u32[]{:S(2)}) copy-start(bf16[64,1408]{1,0:T(8,128)(2,1)} %param.16) | copy-start | bytes 540676
  1.6 28.2 %all-to-all-start.1 = ((bf16[8,2,512]{2,1,0:T(2,128)(2,1)}), bf16[8,2,512]{2,1,0:T(2,128)(2,1)S(1)}, u32[]{:S(2)}, u32[]{:S(2)}) async-start(bf16[8,2,512]{2,1,0:T(2,128)(2,1)} %reshape.222), calls=%async_computation.1 | async-start | bytes 32768 | tf_op jit(solution)/shard_map/all_to_all | solution.py:92
  26.2 44.1 %copy-start.3 = (bf16[512,128]{1,0:T(8,128)(2,1)}, bf16[512,128]{1,0:T(8,128)(2,1)S(1)}, u32[]{:S(2)}) copy-start(bf16[512,128]{1,0:T(8,128)(2,1)S(1)} %all_gather.3) | copy-start | bytes 393220
  26.2 3.5 copy-start.6
  30.4 9.1 %all-to-all-start.2 = ((bf16[8,64,128]{2,1,0:T(8,128)(2,1)}), bf16[8,64,128]{2,1,0:T(8,128)(2,1)S(1)}, u32[]{:S(2)}, u32[]{:S(2)}) async-start(bf16[8,64,128]{2,1,0:T(8,128)(2,1)} %stack.32), calls=%async_computation.2 | async-start | bytes 262144 | tf_op jit(solution)/shard_map/all_to_all | solution.py:97
  39.5 10.7 %all-to-all-start = ((bf16[64,8,176]{2,0,1:T(8,128)(2,1)}), bf16[64,8,176]{2,0,1:T(8,128)(2,1)S(1)}, u32[]{:S(2)}, u32[]{:S(2)}) async-start(bf16[64,8,176]{2,0,1:T(8,128)(2,1)} %copy.44), calls=%async_computation | async-start | bytes 524288 | tf_op jit(solution)/shard_map/all_to_all | solution.py:91
  43.9 10.7 %collective-permute-start.1 = (bf16[16]{0:T(256)(128)(2,1)S(1)}, bf16[16]{0:T(256)(128)(2,1)S(1)}, u32[]{:S(2)}, u32[]{:S(2)}) collective-permute-start(bf16[16]{0:T(256)(128)(2,1)S(1)} %convert_element_type.166), channel_id=1, source_target_pairs={{0,8},{8,0},{16,24},{24,16},{32,40},{40,32},{48,56},{56,48},{64,72... | collective-permute-start | bytes 104 | tf_op jit(solution)/shard_map/ppermute | solution.py:14
  50.2 21.8 %all-to-all-start.3 = ((bf16[64,8,1024]{2,0,1:T(8,128)(2,1)}), bf16[64,8,1024]{2,0,1:T(8,128)(2,1)S(1)}, u32[]{:S(2)}, u32[]{:S(2)}) async-start(bf16[64,8,1024]{2,0,1:T(8,128)(2,1)} %bitcast.123), calls=%async_computation.3 | async-start | bytes 2097152 | tf_op jit(solution)/shard_map/all_to_all | solution.py:90
  54.7 5.5 %collective-permute-start.3 = (bf16[16]{0:T(256)(128)(2,1)S(1)}, bf16[16]{0:T(256)(128)(2,1)S(1)}, u32[]{:S(2)}, u32[]{:S(2)}) collective-permute-start(bf16[16]{0:T(256)(128)(2,1)S(1)} %fusion.63), channel_id=1, source_target_pairs={{0,16},{8,24},{16,0},{24,8},{32,48},{40,56},{48,32},{56,40},{64,80... | collective-permute-start | bytes 104 | tf_op jit(solution)/shard_map/ppermute | solution.py:14
  60.2 8.2 %collective-permute-start.5 = (bf16[16]{0:T(256)(128)(2,1)S(1)}, bf16[16]{0:T(256)(128)(2,1)S(1)}, u32[]{:S(2)}, u32[]{:S(2)}) collective-permute-start(bf16[16]{0:T(256)(128)(2,1)S(1)} %convert_element_type.176), channel_id=1, source_target_pairs={{0,32},{8,40},{16,48},{24,56},{32,0},{40,8},{48,16},{56,24},{64,96... | collective-permute-start | bytes 104 | tf_op jit(solution)/shard_map/ppermute | solution.py:14
  68.4 171.3 %collective-permute-start.7 = (bf16[16]{0:T(256)(128)(2,1)S(1)}, bf16[16]{0:T(256)(128)(2,1)S(1)}, u32[]{:S(2)}, u32[]{:S(2)}) collective-permute-start(bf16[16]{0:T(256)(128)(2,1)S(1)} %convert_element_type.181), channel_id=1, source_target_pairs={{0,64},{8,72},{16,80},{24,88},{32,96},{40,104},{48,112},{56,120},{... | collective-permute-start | bytes 104 | tf_op jit(solution)/shard_map/ppermute | solution.py:14
  71.9 1.0 copy-start.2
  236.7 25.7 %copy-start.1 = (f32[16,128,64]{1,2,0:T(8,128)S(1)}, f32[16,128,64]{1,2,0:T(8,128)}, u32[]{:S(2)}) copy-start(f32[16,128,64]{1,2,0:T(8,128)} %get-tuple-element.111) | copy-start | bytes 1572868
  236.7 32.6 %copy-start.7 = (f32[128]{0:T(128)S(1)}, f32[128]{0:T(128)}, u32[]{:S(2)}) copy-start(f32[128]{0:T(128)} %param.17) | copy-start | bytes 1540
  237.8 7.8 %collective-permute-start = (bf16[16,128,64]{1,2,0:T(8,128)(2,1)S(1)}, bf16[16,128,64]{1,2,0:T(8,128)(2,1)S(1)}, u32[]{:S(2)}, u32[]{:S(2)}) collective-permute-start(bf16[16,128,64]{1,2,0:T(8,128)(2,1)S(1)} %convert_element_type.163), channel_id=1, source_target_pairs={{0,8},{8,0},{16,24},{24,16},{32,40},{40,32},{48,56},{56,48},{64,72... | collective-permute-start | bytes 786440 | tf_op jit(solution)/shard_map/ppermute | solution.py:14
  239.8 5.8 %collective-permute-start.9 = (bf16[16]{0:T(256)(128)(2,1)S(1)}, bf16[16]{0:T(256)(128)(2,1)S(1)}, u32[]{:S(2)}, u32[]{:S(2)}) collective-permute-start(bf16[16]{0:T(256)(128)(2,1)S(1)} %get-tuple-element.258), channel_id=1, source_target_pairs={{0,128},{8,136},{16,144},{24,152},{32,160},{40,168},{48,176},{56,1... | collective-permute-start | bytes 104 | tf_op jit(solution)/shard_map/ppermute | solution.py:14
  246.9 15.5 %collective-permute-start.2 = (bf16[16,128,64]{1,2,0:T(8,128)(2,1)S(1)}, bf16[16,128,64]{1,2,0:T(8,128)(2,1)S(1)}, u32[]{:S(2)}, u32[]{:S(2)}) collective-permute-start(bf16[16,128,64]{1,2,0:T(8,128)(2,1)S(1)} %fusion.68), channel_id=1, source_target_pairs={{0,16},{8,24},{16,0},{24,8},{32,48},{40,56},{48,32},{56,40},{64,80... | collective-permute-start | bytes 786440 | tf_op jit(solution)/shard_map/ppermute | solution.py:14
  262.7 18.1 %collective-permute-start.4 = (bf16[16,128,64]{1,2,0:T(8,128)(2,1)S(1)}, bf16[16,128,64]{1,2,0:T(8,128)(2,1)S(1)}, u32[]{:S(2)}, u32[]{:S(2)}) collective-permute-start(bf16[16,128,64]{1,2,0:T(8,128)(2,1)S(1)} %fusion.67), channel_id=1, source_target_pairs={{0,32},{8,40},{16,48},{24,56},{32,0},{40,8},{48,16},{56,24},{64,96... | collective-permute-start | bytes 786440 | tf_op jit(solution)/shard_map/ppermute | solution.py:14
  281.3 7.7 %collective-permute-start.6 = (bf16[16,128,64]{1,2,0:T(8,128)(2,1)S(1)}, bf16[16,128,64]{1,2,0:T(8,128)(2,1)S(1)}, u32[]{:S(2)}, u32[]{:S(2)}) collective-permute-start(bf16[16,128,64]{1,2,0:T(8,128)(2,1)S(1)} %get-tuple-element.253), channel_id=1, source_target_pairs={{0,64},{8,72},{16,80},{24,88},{32,96},{40,104},{48,112},{56,120},{... | collective-permute-start | bytes 786440 | tf_op jit(solution)/shard_map/ppermute | solution.py:14
  289.2 15.2 %collective-permute-start.8 = (bf16[16,128,64]{1,2,0:T(8,128)(2,1)S(1)}, bf16[16,128,64]{1,2,0:T(8,128)(2,1)S(1)}, u32[]{:S(2)}, u32[]{:S(2)}) collective-permute-start(bf16[16,128,64]{1,2,0:T(8,128)(2,1)S(1)} %fusion.66), channel_id=1, source_target_pairs={{0,128},{8,136},{16,144},{24,152},{32,160},{40,168},{48,176},{56,1... | collective-permute-start | bytes 786440 | tf_op jit(solution)/shard_map/ppermute | solution.py:14
  293.6 29.9 %copy-start.4 = (bf16[512,128]{1,0:T(8,128)(2,1)S(1)}, bf16[512,128]{1,0:T(8,128)(2,1)}, u32[]{:S(2)}) copy-start(bf16[512,128]{1,0:T(8,128)(2,1)} %copy-done.3) | copy-start | bytes 393220
  304.7 17.4 %collective-permute-start.10 = (bf16[16,128,64]{1,2,0:T(8,128)(2,1)S(1)}, bf16[16,128,64]{1,2,0:T(8,128)(2,1)S(1)}, u32[]{:S(2)}, u32[]{:S(2)}) collective-permute-start(bf16[16,128,64]{1,2,0:T(8,128)(2,1)S(1)} %fusion.42), channel_id=1, source_target_pairs={{0,256},{8,264},{16,272},{24,280},{32,288},{40,296},{48,304},{56,3... | collective-permute-start | bytes 786440 | tf_op jit(solution)/shard_map/ppermute | solution.py:14
  322.3 1.1 copy-start.5
